TPU v7x, 256 devices: a whole 4x4x8 slice. The times are simulated.
256 devices in a mesh: col: 64 (over z, x, core), row: 4 (over y).
Axes of the slice: x: 4, y: 4, z: 8, core: 2. Of those that a mesh axis runs over, the one named last changes fastest.
Arguments:
- matrix: float32 [16, 512, 1, 8192], P(None, 'row', None, 'col'), may hold values from -1 to 5, as said below
- inverse_factors: float32 [2, 512, 512], replicated, may hold values from -1 to 1, as said below
Outputs:
- factored: float32 [16, 512, 1, 8192], P(None, 'row', None, 'col')
Inputs may be any that keep to these rules, and one draw needn't show every extreme that they name: matrix holds a symmetric matrix. Each inverse_factors[k] is lower triangular with a positive diagonal; it is given independently of matrix.
All inputs are finite; a program needn't handle non-finite values.
Results may differ from a plain program's by a relative error of at most 0.0001.
Values sent between devices are 32-bit elements; how exact they have to be, the bound alone decides.
No kernel may reach another device: no remote copies, remote signals or barrier semaphores. Data moves between devices by JAX's collectives and lax.ppermute only.
A program may use at most 64 MiB of HBM per device.

v0:
```python
import jax
import jax.numpy as jnp
from jax import lax
from jax.sharding import PartitionSpec as P


def broadcast(x, axis, root):
    mine = lax.axis_index(axis) == root
    return lax.psum(jnp.where(mine, x, jnp.zeros_like(x)), axis)


def exact_dot(left_side, right_side):
    return jnp.dot(
        left_side, right_side, precision=lax.Precision.HIGHEST, preferred_element_type=jnp.float32
    )


def shards(matrix, inverse_factors):
    col_count = lax.axis_size("col")
    row_count = lax.axis_size("row")
    col_index = lax.axis_index("col")
    row_index = lax.axis_index("row")
    row_blocks, block_cols, cycles, _ = matrix.shape
    panel_width = inverse_factors.shape[1]
    per_panel = panel_width // block_cols
    local_rows = row_blocks * block_cols
    square_view = matrix.reshape(local_rows, cycles * block_cols)
    global_rows = (
        (jnp.arange(row_blocks)[:, None] * row_count + row_index) * block_cols
        + jnp.arange(block_cols)[None, :]
    ).reshape(-1)
    take_index = (jnp.arange(cycles) * col_count + col_index) // row_count
    row_root = col_index % row_count

    def masked(factor_cols, offset):
        return jnp.where(global_rows[:, None] >= offset, factor_cols, 0.0)

    current = square_view
    for panel in range(2):
        factor = inverse_factors[panel]
        pieces = [
            broadcast(current, "col", panel * per_panel + member) for member in range(per_panel)
        ]
        factor_cols = exact_dot(jnp.concatenate(pieces, axis=1), factor.T)
        trailing = masked(factor_cols, (panel + 1) * panel_width)
        blocked = trailing.reshape(row_blocks, block_cols, panel_width)
        picked = jnp.take(blocked, take_index, axis=0).reshape(cycles * block_cols, panel_width)
        gathered = lax.all_gather(picked, "row", axis=0, tiled=True)
        column_part = lax.dynamic_slice_in_dim(
            gathered, row_root * picked.shape[0], picked.shape[0], 0
        )
        current = current - exact_dot(trailing, column_part.T)
        place_factor_cols = masked(factor_cols, panel * panel_width)
        offset_id = col_index - panel * per_panel
        inside = (offset_id >= 0) & (offset_id < per_panel)
        position = jnp.clip(offset_id, 0, per_panel - 1)
        chosen = lax.dynamic_slice_in_dim(place_factor_cols, position * block_cols, block_cols, 1)
        leading = jnp.where(inside, chosen, current)
        current = jnp.concatenate([leading, current[:, block_cols:]], axis=1)
    return current.reshape(row_blocks, block_cols, cycles, block_cols)


def solution(mesh):
    return jax.shard_map(
        shards,
        mesh=mesh,
        in_specs=(P(None, "row", None, "col"), P()),
        out_specs=P(None, "row", None, "col"),
        check_vma=False,
    )
```

profile of v0, /device:TPU:2, one launch (start us, length us, event | category | flops | bytes accessed | tf_op | source)
XLA Modules:
  0.0 504.0 jit_solution(6828557385005431134)
XLA Ops:
  6.5 0.0 all-reduce.7.cloned.1.call-start
  6.5 0.0 copy-start.3
  6.5 3.4 broadcast_select_fusion.9
  10.0 0.0 all-reduce.7.cloned.1.call-update
  10.0 0.0 all-gather.5.cloned.1.call-start
  10.1 0.1 fusion.31
  10.2 199.4 %all-reduce.7.cloned.1.call-done = (f32[2048,128]{1,0:T(8,128)}, f32[2048,128]{1,0:T(8,128)}, f32[2048,128]{1,0:T(8,128)}, f32[2048,128]{1,0:T(8,128)}) async-done(((f32[2048,128]{1,0:T(8,128)}, f32[2048,128]{1,0:T(8,128)}, f32[2048,128]{1,0:T(8,128)}, f32[2048,128]{1,0:T(8,128)}), (f32[2048,128]{1,0:T(8,128)}, f32[2048,128]{1,0:T(8,128)}, f32[2048,128]{1,0:T(8,128)}, ...) | async-done | bytes 4194320 | tf_op jit(solution)/shard_map/psum | solution.py:9
  209.6 0.0 copy-done.3
  209.6 0.0 copy-start.2
  209.6 9.9 %broadcast_select_fusion = (f32[2048,512]{1,0:T(8,128)S(1)}, f32[2048,512]{1,0:T(8,128)}) fusion(pred[2048]{0:T(1024)(128)(4,1)S(1)} %get-tuple-element.35, f32[2,512,512]{2,1,0:T(8,128)S(1)} %copy-done.3, f32[2048,128]{1,0:T(8,128)} %get-tuple-element.21, f32[2048,128]{1,0:T(8,128)} %get-tuple-element.22, f32[2048,128]{1,0:T(8,128)} %get-tuple-element.23, ...), kind=kOutput, calls=%fused_computation.20 | convolution fusion | flops 6446645248 | bytes 13633536 | tf_op jit(solution)/shard_map/dot_general | solution.py:13
  219.5 0.0 copy-start
  219.5 2.0 copy-done
  221.5 0.7 dynamic-slice_select_fusion.3
  222.2 0.0 all-gather.5.cloned.1.call-update
  222.2 0.0 all-reduce.5.cloned.1.call-start
  222.3 25.7 %all-gather.5.cloned.1.call-done = f32[1,512,512]{2,1,0:T(8,128)} async-done(((f32[1,128,512]{2,1,0:T(8,128)}), f32[1,512,512]{2,1,0:T(8,128)}) %all-gather.5.cloned.1.call-update) | async-done | bytes 1048592 | tf_op jit(solution)/shard_map/all_gather | solution.py:48
  248.0 0.0 copy-done.2
  248.0 8.0 %broadcast_select_fusion.5 = (f32[2048,128]{1,0:T(8,128)}, f32[2048,128]{1,0:T(8,128)}, f32[2048,128]{1,0:T(8,128)}, f32[2048,128]{1,0:T(8,128)}, f32[2048,128]{1,0:T(8,128)S(1)}) fusion(pred[]{:T(512)S(6)} %eq.26, pred[]{:T(512)S(6)} %eq.33, pred[]{:T(512)S(6)} %eq.32, pred[]{:T(512)S(6)} %eq.31, f32[2048,128]{1,0:T(8,128)S(1)} %bitcast.40, ...), kind=kOutput, calls=%fused_computation.31 | convolution fusion | flops 1612447744 | bytes 11798541 | tf_op jit(solution)/shard_map/dot_general | solution.py:13
  256.0 0.0 all-reduce.5.cloned.1.call-update
  256.0 0.2 all-gather.7.cloned.1.call-start
  256.3 195.5 %all-reduce.5.cloned.1.call-done = (f32[2048,128]{1,0:T(8,128)}, f32[2048,128]{1,0:T(8,128)}, f32[2048,128]{1,0:T(8,128)}, f32[2048,128]{1,0:T(8,128)}) async-done(((f32[2048,128]{1,0:T(8,128)}, f32[2048,128]{1,0:T(8,128)}, f32[2048,128]{1,0:T(8,128)}, f32[2048,128]{1,0:T(8,128)}), (f32[2048,128]{1,0:T(8,128)}, f32[2048,128]{1,0:T(8,128)}, f32[2048,128]{1,0:T(8,128)}, ...) | async-done | bytes 4194320 | tf_op jit(solution)/shard_map/psum | solution.py:9
  451.7 10.3 %broadcast_select_fusion.1 = (f32[2048,512]{1,0:T(8,128)S(1)}, f32[2048,512]{1,0:T(8,128)}) fusion(pred[2048]{0:T(1024)(128)(4,1)S(1)} %get-tuple-element.33, f32[2,512,512]{2,1,0:T(8,128)} %param.5, f32[2048,128]{1,0:T(8,128)} %get-tuple-element.17, f32[2048,128]{1,0:T(8,128)} %get-tuple-element.18, f32[2048,128]{1,0:T(8,128)} %get-tuple-element.19, ...), kind=kOutput, calls=%fused_computation.21 | convolution fusion | flops 6446645248 | bytes 13633536 | tf_op jit(solution)/shard_map/dot_general | solution.py:13
  462.0 0.0 copy-start.1
  462.0 2.0 copy-done.1
  464.0 0.7 dynamic-slice_select_fusion.2
  464.7 0.0 all-gather.7.cloned.1.call-update
  464.8 25.7 %all-gather.7.cloned.1.call-done = f32[1,512,512]{2,1,0:T(8,128)} async-done(((f32[1,128,512]{2,1,0:T(8,128)}), f32[1,512,512]{2,1,0:T(8,128)}) %all-gather.7.cloned.1.call-update) | async-done | bytes 1048592 | tf_op jit(solution)/shard_map/all_gather | solution.py:48
  490.5 7.0 %fusion.16 = f32[2048,128]{1,0:T(8,128)} fusion(f32[2048,128]{1,0:T(8,128)S(1)} %get-tuple-element.38, f32[2048,512]{1,0:T(8,128)} %copy-done.1, f32[2048,512]{1,0:T(8,128)} %get-tuple-element.40, s32[]{:T(128)S(6)} %select_n.137, pred[2048]{0:T(1024)(128)(4,1)S(1)} %get-tuple-element.35, pred[]{:T(512)S(6)} %and.21, ...), kind=kOutput, calls=%fused_computation.17 | convolution fusion | flops 1611399168 | bytes 7604233 | tf_op jit(solution)/shard_map/dot_general | solution.py:13
  (1 shorter events, 0.0 us)
Async XLA Ops:
  6.5 203.1 %all-reduce.7.cloned.1.call-start = ((), (), s32[]{:S(2)}) async-start(), calls=%async_computation.3 | async-start | bytes 8388608 | tf_op jit(solution)/shard_map/psum | solution.py:9
  6.5 203.1 %copy-start.3 = (f32[2,512,512]{2,1,0:T(8,128)S(1)}, f32[2,512,512]{2,1,0:T(8,128)}, u32[]{:S(2)}) copy-start(f32[2,512,512]{2,1,0:T(8,128)} %param.5) | copy-start | bytes 6291460
  10.0 238.0 %all-gather.5.cloned.1.call-start = ((), (), s32[]{:S(2)}) async-start(), calls=%async_computation | async-start | bytes 1310720 | tf_op jit(solution)/shard_map/all_gather | solution.py:48
  209.6 38.4 %copy-start.2 = (f32[16,128,1,128]{3,2,1,0:T(1,128)S(1)}, f32[16,128,1,128]{3,2,1,0:T(1,128)}, u32[]{:S(2)}) copy-start(f32[16,128,1,128]{3,2,1,0:T(1,128)} %param.4) | copy-start | bytes 3145732
  219.5 2.0 copy-start
  222.2 229.5 %all-reduce.5.cloned.1.call-start = ((), (), s32[]{:S(2)}) async-start(), calls=%async_computation.2 | async-start | bytes 8388608 | tf_op jit(solution)/shard_map/psum | solution.py:9
  256.0 234.5 %all-gather.7.cloned.1.call-start = ((), (), s32[]{:S(2)}) async-start(), calls=%async_computation.1 | async-start | bytes 1310720 | tf_op jit(solution)/shard_map/all_gather | solution.py:48
  462.0 2.0 copy-start.1
Sparse Core Ops, SparseCore 0:
  11.3 198.2 all-reduce.6
  222.3 25.5 all-gather.4
  256.1 195.5 all-reduce.4
  464.9 25.5 all-gather.6
where the time goes:
time: 504 us
  waiting for transfers between devices  446 us (88%)
  matrix products  35.2 us (7%)
  between operations  13.2 us (3%)
    psum x2, waiting for transfers between devices, broadcast(): return lax.psum(jnp.where(mine, x, jnp.zeros_like(x)), axis)  395 us
    all_gather x2, waiting for transfers between devices, shards(): gathered = lax.all_gather(picked, 'row', axis=0, tiled=True)  51.4 us
    dot_general x4, matrix products, exact_dot(): jnp.dot(left_side, right_side, precision=lax.Precision.HIGHEST, preferred...  35.2 us
  transfers between devices with their start and end apart: 4, of which 4 were waited for; matrix products, arithmetic and copies ran while one was open for 0% of the time, Pallas kernels for 0%

commit v1 on v0

--- a/solution.py
+++ b/solution.py
@@ -45,7 +45,31 @@
         trailing = masked(factor_cols, (panel + 1) * panel_width)
         blocked = trailing.reshape(row_blocks, block_cols, panel_width)
         picked = jnp.take(blocked, take_index, axis=0).reshape(cycles * block_cols, panel_width)
-        gathered = lax.all_gather(picked, "row", axis=0, tiled=True)
+        everything = lax.axis_size("row")
+        part_now, extra, z_new = (everything, lax.axis_index("row"), picked.shape[0])
+        in_order = []
+        for kk, dd in enumerate(picked.shape):
+            in_order.append(dd * part_now if kk == 0 else dd)
+        gathered = lax.dynamic_update_slice_in_dim(
+            jnp.zeros(in_order, picked.dtype), picked, extra * z_new, axis=0
+        )
+        t_next = k_now = picked
+        for to_i in range(1, part_now // 2 + 1):
+            rack = []
+            for kk in range(part_now):
+                rack.append((kk, (kk + 1) % part_now))
+            t_next = lax.ppermute(t_next, axis_name="row", perm=rack)
+            gathered = lax.dynamic_update_slice_in_dim(
+                gathered, t_next, (extra - to_i) % part_now * z_new, axis=0
+            )
+            if 2 * to_i < part_now:
+                found = []
+                for kk in range(part_now):
+                    found.append((kk, (kk - 1) % part_now))
+                k_now = lax.ppermute(k_now, axis_name="row", perm=found)
+                gathered = lax.dynamic_update_slice_in_dim(
+                    gathered, k_now, (extra + to_i) % part_now * z_new, axis=0
+                )
         column_part = lax.dynamic_slice_in_dim(
             gathered, row_root * picked.shape[0], picked.shape[0], 0
         )

time: 504 us -> 482 us (0.956)
  waiting for transfers between devices: 446 us -> 418 us
  starting transfers between devices: 0.31 us -> 7.22 us
    all_gather x2 -> x0, waiting for transfers between devices: 51.4 us -> none  [shards(): gathered = lax.all_gather(picked, 'row', axis=0, tiled=True)]
    ppermute x0 -> x6, waiting for transfers between devices: none -> 23.7 us  [the longest x4 23.7 us: shards(): t_next = lax.ppermute(t_next, axis_name='row', perm=rack)]
    ppermute x0 -> x6, starting transfers between devices: none -> 7.18 us  [the longest x4 3.67 us: shards(): t_next = lax.ppermute(t_next, axis_name='row', perm=rack)]
  transfers between devices with their start and end apart: 4 -> 8, of which waited for: 4 -> 6; matrix products, arithmetic and copies ran while one was open for 0% -> 0% of each run, Pallas kernels for 0% -> 0%
where the time goes in v1:
time: 482 us; the launch traced here: 481 us
  waiting for transfers between devices  418 us (87%)
  matrix products  34.9 us (7%)
  between operations  13.5 us (3%)
  starting transfers between devices  7.22 us (1%)
    psum x2, waiting for transfers between devices, broadcast(): return lax.psum(jnp.where(mine, x, jnp.zeros_like(x)), axis)  394 us
    dot_general x4, matrix products, exact_dot(): jnp.dot(left_side, right_side, precision=lax.Precision.HIGHEST, preferred...  34.9 us
    ppermute x4, waiting for transfers between devices, shards(): t_next = lax.ppermute(t_next, axis_name='row', perm=rack)  23.7 us
  transfers between devices with their start and end apart: 8, of which 6 were waited for; matrix products, arithmetic and copies ran while one was open for 0% of the time, Pallas kernels for 0%

profile of v1, /device:TPU:2, one launch (start us, length us, event | category | flops | bytes accessed | tf_op | source)
XLA Modules:
  0.0 481.0 jit_solution(13205620879647082422)
XLA Ops:
  6.5 0.0 all-reduce.7.cloned.1.call-start
  6.5 0.0 copy-start.3
  6.5 3.5 broadcast_select_fusion.9
  10.0 0.0 all-reduce.7.cloned.1.call-update
  10.0 0.0 all-reduce.5.cloned.1.call-start
  10.1 0.1 fusion.29
  10.2 199.4 %all-reduce.7.cloned.1.call-done = (f32[2048,128]{1,0:T(8,128)}, f32[2048,128]{1,0:T(8,128)}, f32[2048,128]{1,0:T(8,128)}, f32[2048,128]{1,0:T(8,128)}) async-done(((f32[2048,128]{1,0:T(8,128)}, f32[2048,128]{1,0:T(8,128)}, f32[2048,128]{1,0:T(8,128)}, f32[2048,128]{1,0:T(8,128)}), (f32[2048,128]{1,0:T(8,128)}, f32[2048,128]{1,0:T(8,128)}, f32[2048,128]{1,0:T(8,128)}, ...) | async-done | bytes 4194320 | tf_op jit(solution)/shard_map/psum | solution.py:9
  209.6 0.0 copy-done.3
  209.6 9.8 %broadcast_select_fusion = (f32[2048,512]{1,0:T(8,128)S(1)}, f32[2048,512]{1,0:T(8,128)}) fusion(pred[2048]{0:T(1024)(128)(4,1)S(1)} %get-tuple-element.39, f32[2,512,512]{2,1,0:T(8,128)S(1)} %copy-done.3, f32[2048,128]{1,0:T(8,128)} %get-tuple-element.21, f32[2048,128]{1,0:T(8,128)} %get-tuple-element.22, f32[2048,128]{1,0:T(8,128)} %get-tuple-element.23, ...), kind=kOutput, calls=%fused_computation.20 | convolution fusion | flops 6446645248 | bytes 13633536 | tf_op jit(solution)/shard_map/dot_general | solution.py:13
  219.4 0.0 copy-start
  219.4 0.0 copy-start.2
  219.4 0.1 broadcast.86.clone
  219.5 1.9 copy-done
  221.4 0.1 constant_dynamic-update-slice_fusion.7
  221.4 1.6 collective-permute-start
  223.0 1.8 collective-permute-start.1
  224.8 4.6 collective-permute-done
  229.4 0.3 collective-permute-start.2
  229.7 0.0 collective-permute-done.1
  229.7 7.2 %collective-permute-done.2 = f32[128,512]{1,0:T(8,128)S(1)} collective-permute-done((f32[128,512]{1,0:T(8,128)S(1)}, f32[128,512]{1,0:T(8,128)S(1)}, u32[]{:S(2)}, u32[]{:S(2)}) %collective-permute-start.2) | collective-permute-done | bytes 262176 | tf_op jit(solution)/shard_map/ppermute | solution.py:61
  237.0 0.0 copy-done.2
  237.0 8.0 %broadcast_select_fusion.5 = (f32[2048,128]{1,0:T(8,128)}, f32[2048,128]{1,0:T(8,128)}, f32[2048,128]{1,0:T(8,128)}, f32[2048,128]{1,0:T(8,128)}, f32[2048,128]{1,0:T(8,128)S(1)}) fusion(pred[]{:T(512)S(6)} %eq.32, pred[]{:T(512)S(6)} %eq.39, pred[]{:T(512)S(6)} %eq.38, pred[]{:T(512)S(6)} %eq.37, f32[2048,128]{1,0:T(8,128)S(1)} %bitcast.38, ...), kind=kOutput, calls=%fused_computation.31 | convolution fusion | flops 1612447744 | bytes 11798541 | tf_op jit(solution)/shard_map/dot_general | solution.py:13
  244.9 0.0 all-reduce.5.cloned.1.call-update
  245.0 194.4 %all-reduce.5.cloned.1.call-done = (f32[2048,128]{1,0:T(8,128)}, f32[2048,128]{1,0:T(8,128)}, f32[2048,128]{1,0:T(8,128)}, f32[2048,128]{1,0:T(8,128)}) async-done(((f32[2048,128]{1,0:T(8,128)}, f32[2048,128]{1,0:T(8,128)}, f32[2048,128]{1,0:T(8,128)}, f32[2048,128]{1,0:T(8,128)}), (f32[2048,128]{1,0:T(8,128)}, f32[2048,128]{1,0:T(8,128)}, f32[2048,128]{1,0:T(8,128)}, ...) | async-done | bytes 4194320 | tf_op jit(solution)/shard_map/psum | solution.py:9
  439.4 10.3 %broadcast_select_fusion.1 = (f32[2048,512]{1,0:T(8,128)S(1)}, f32[2048,512]{1,0:T(8,128)}) fusion(pred[2048]{0:T(1024)(128)(4,1)S(1)} %get-tuple-element.37, f32[2,512,512]{2,1,0:T(8,128)} %param.5, f32[2048,128]{1,0:T(8,128)} %get-tuple-element.17, f32[2048,128]{1,0:T(8,128)} %get-tuple-element.18, f32[2048,128]{1,0:T(8,128)} %get-tuple-element.19, ...), kind=kOutput, calls=%fused_computation.21 | convolution fusion | flops 6446645248 | bytes 13633536 | tf_op jit(solution)/shard_map/dot_general | solution.py:13
  449.6 0.0 copy-start.1
  449.6 0.1 broadcast.86
  449.8 1.9 copy-done.1
  451.6 0.1 constant_dynamic-update-slice_fusion.3
  451.7 1.6 collective-permute-start.3
  453.2 1.8 collective-permute-start.4
  455.0 4.6 collective-permute-done.3
  459.6 0.3 collective-permute-start.5
  459.9 0.0 collective-permute-done.4
  459.9 7.2 %collective-permute-done.5 = f32[128,512]{1,0:T(8,128)S(1)} collective-permute-done((f32[128,512]{1,0:T(8,128)S(1)}, f32[128,512]{1,0:T(8,128)S(1)}, u32[]{:S(2)}, u32[]{:S(2)}) %collective-permute-start.5) | collective-permute-done | bytes 262176 | tf_op jit(solution)/shard_map/ppermute | solution.py:61
  467.2 6.9 %fusion.16 = f32[2048,128]{1,0:T(8,128)} fusion(f32[2048,128]{1,0:T(8,128)S(1)} %get-tuple-element.42, f32[2048,512]{1,0:T(8,128)} %copy-done.1, f32[2048,512]{1,0:T(8,128)} %get-tuple-element.44, s32[]{:T(128)S(6)} %select_n.178, pred[2048]{0:T(1024)(128)(4,1)S(1)} %get-tuple-element.39, pred[]{:T(512)S(6)} %and.36, ...), kind=kOutput, calls=%fused_computation.17 | convolution fusion | flops 1611399168 | bytes 7604233 | tf_op jit(solution)/shard_map/dot_general | solution.py:13
  (7 shorter events, 0.1 us)
Async XLA Ops:
  6.5 203.1 %all-reduce.7.cloned.1.call-start = ((), (), s32[]{:S(2)}) async-start(), calls=%async_computation.1 | async-start | bytes 8388608 | tf_op jit(solution)/shard_map/psum | solution.py:9
  6.5 203.1 %copy-start.3 = (f32[2,512,512]{2,1,0:T(8,128)S(1)}, f32[2,512,512]{2,1,0:T(8,128)}, u32[]{:S(2)}) copy-start(f32[2,512,512]{2,1,0:T(8,128)} %param.5) | copy-start | bytes 6291460
  10.0 429.3 %all-reduce.5.cloned.1.call-start = ((), (), s32[]{:S(2)}) async-start(), calls=%async_computation | async-start | bytes 8388608 | tf_op jit(solution)/shard_map/psum | solution.py:9
  219.4 2.0 copy-start
  219.4 17.6 %copy-start.2 = (f32[16,128,1,128]{3,2,1,0:T(1,128)S(1)}, f32[16,128,1,128]{3,2,1,0:T(1,128)}, u32[]{:S(2)}) copy-start(f32[16,128,1,128]{3,2,1,0:T(1,128)} %param.4) | copy-start | bytes 3145732
  221.4 7.9 %collective-permute-start = (f32[128,512]{1,0:T(8,128)S(1)}, f32[128,512]{1,0:T(8,128)S(1)}, u32[]{:S(2)}, u32[]{:S(2)}) collective-permute-start(f32[128,512]{1,0:T(8,128)S(1)} %get-tuple-element.28), channel_id=1, source_target_pairs={{0,1},{1,2},{2,3},{3,0},{4,5},{5,6},{6,7},{7,4},{8,9},{9,10},{10,1... | collective-permute-start | bytes 786440 | tf_op jit(solution)/shard_map/ppermute | solution.py:61
  223.0 6.7 %collective-permute-start.1 = (f32[128,512]{1,0:T(8,128)S(1)}, f32[128,512]{1,0:T(8,128)S(1)}, u32[]{:S(2)}, u32[]{:S(2)}) collective-permute-start(f32[128,512]{1,0:T(8,128)S(1)} %get-tuple-element.28), channel_id=1, source_target_pairs={{0,3},{1,0},{2,1},{3,2},{4,7},{5,4},{6,5},{7,6},{8,11},{9,8},{10,9... | collective-permute-start | bytes 786440 | tf_op jit(solution)/shard_map/ppermute | solution.py:69
  229.4 7.6 %collective-permute-start.2 = (f32[128,512]{1,0:T(8,128)S(1)}, f32[128,512]{1,0:T(8,128)S(1)}, u32[]{:S(2)}, u32[]{:S(2)}) collective-permute-start(f32[128,512]{1,0:T(8,128)S(1)} %collective-permute-done), channel_id=1, source_target_pairs={{0,1},{1,2},{2,3},{3,0},{4,5},{5,6},{6,7},{7,4},{8,9},{9,10},{10,1... | collective-permute-start | bytes 786440 | tf_op jit(solution)/shard_map/ppermute | solution.py:61
  449.6 2.0 copy-start.1
  451.7 7.9 %collective-permute-start.3 = (f32[128,512]{1,0:T(8,128)S(1)}, f32[128,512]{1,0:T(8,128)S(1)}, u32[]{:S(2)}, u32[]{:S(2)}) collective-permute-start(f32[128,512]{1,0:T(8,128)S(1)} %get-tuple-element.26), channel_id=1, source_target_pairs={{0,1},{1,2},{2,3},{3,0},{4,5},{5,6},{6,7},{7,4},{8,9},{9,10},{10,1... | collective-permute-start | bytes 786440 | tf_op jit(solution)/shard_map/ppermute | solution.py:61
  453.2 6.7 %collective-permute-start.4 = (f32[128,512]{1,0:T(8,128)S(1)}, f32[128,512]{1,0:T(8,128)S(1)}, u32[]{:S(2)}, u32[]{:S(2)}) collective-permute-start(f32[128,512]{1,0:T(8,128)S(1)} %get-tuple-element.26), channel_id=1, source_target_pairs={{0,3},{1,0},{2,1},{3,2},{4,7},{5,4},{6,5},{7,6},{8,11},{9,8},{10,9... | collective-permute-start | bytes 786440 | tf_op jit(solution)/shard_map/ppermute | solution.py:69
  459.6 7.6 %collective-permute-start.5 = (f32[128,512]{1,0:T(8,128)S(1)}, f32[128,512]{1,0:T(8,128)S(1)}, u32[]{:S(2)}, u32[]{:S(2)}) collective-permute-start(f32[128,512]{1,0:T(8,128)S(1)} %collective-permute-done.3), channel_id=1, source_target_pairs={{0,1},{1,2},{2,3},{3,0},{4,5},{5,6},{6,7},{7,4},{8,9},{9,10},{10,1... | collective-permute-start | bytes 786440 | tf_op jit(solution)/shard_map/ppermute | solution.py:61
Sparse Core Ops, SparseCore 0:
  11.3 198.2 all-reduce.6
  245.1 194.2 all-reduce.4
